TPU v7x, 128 devices: a whole 4x4x4 slice. The times are simulated.
128 devices in a mesh: lat: 16 (over z, y), lon: 8 (over x, core).
Axes of the slice: x: 4, y: 4, z: 4, core: 2. Of those that a mesh axis runs over, the one named last changes fastest.
Arguments:
- encoder_features: bfloat16 [512, 256, 128], P('lat', 'lon'), may hold values from -6 to 6
- noise: bfloat16 [512, 256, 128], P('lat', 'lon'), may hold values from -6 to 6
- patch_cols: int32 [16, 32], P('lat'), may hold values from 0 to 255, as said below
- timesteps: int32 [16, 32], P('lat'), may hold values from 0 to 31
- w_conv: bfloat16 [1152, 128], replicated, may hold values from -0.1875 to 0.1875
- w_down: bfloat16 [512, 256], replicated, may hold values from -0.25 to 0.25
- w_up: bfloat16 [256, 512], replicated, may hold values from -0.375 to 0.375
- w_out: bfloat16 [128, 128], replicated, may hold values from -0.5 to 0.5
Outputs:
- feature_grad: float32 [512, 256, 128], P('lat', 'lon')
- grad_conv: float32 [1152, 128], replicated
- grad_down: float32 [512, 256], replicated
- grad_up: float32 [256, 512], replicated
- grad_out: float32 [128, 128], replicated
- loss_value: float32 [], replicated
Inputs may be any that keep to these rules, and one draw needn't show every extreme that they name: `patch_cols`: in each band at most 12 patches start in one device's block of 32 longitude cells, and exactly 12 start in one block.
All inputs are finite; a program needn't handle non-finite values.
Results may differ from a plain program's by a relative error of at most 0.009.
Values may be sent and summed in bfloat16 or wider, within the bound.
No kernel may reach another device: no remote copies, remote signals or barrier semaphores. Data moves between devices by JAX's collectives and lax.ppermute only.
A program may use at most 64 MiB of HBM per device.

v0:
```python
import math

import jax
import jax.numpy as jnp
from jax import lax
from jax.sharding import PartitionSpec as P

NSTEPS = 32
PMAX = 12


sigma_low = 0.02
sigma_high = 20.0


def shifted(block, axis, distance):
    devices = range(lax.axis_size(axis))
    route = [((i - distance) % len(devices), i) for i in devices]
    return lax.ppermute(block, axis, route)


def sigma_of(levels):
    return sigma_low * jnp.exp(
        levels.astype(jnp.float32) / (NSTEPS - 1) * math.log(sigma_high / sigma_low)
    )


def patch_loss(feat, noise_patch, sigma, w_conv, w_down, w_up, w_out):
    side = feat.shape[0]
    chans = feat.shape[2]
    scale_in = 1.0 / jnp.sqrt(1.0 + sigma * sigma)
    hidden = (scale_in * (feat + sigma * noise_patch.astype(jnp.float32))).astype(jnp.bfloat16)
    padded = jnp.pad(hidden, ((1, 1), (1, 1), (0, 0)))
    stacked = jnp.concatenate(
        [
            padded[row_off : row_off + side, col_off : col_off + side]
            for row_off in range(3)
            for col_off in range(3)
        ],
        axis=-1,
    ).reshape(side * side, 9 * chans)
    first = jax.nn.silu(jnp.dot(stacked, w_conv, preferred_element_type=jnp.float32)).astype(
        jnp.bfloat16
    )
    coarse_in = (
        first.reshape(side // 2, 2, side // 2, 2, chans)
        .transpose(0, 2, 1, 3, 4)
        .reshape(side * side // 4, 4 * chans)
    )
    coarse = jax.nn.silu(jnp.dot(coarse_in, w_down, preferred_element_type=jnp.float32)).astype(
        jnp.bfloat16
    )
    upward = (
        jnp.dot(coarse, w_up, preferred_element_type=jnp.float32)
        .reshape(side // 2, side // 2, 2, 2, chans)
        .transpose(0, 2, 1, 3, 4)
        .reshape(side * side, chans)
    )
    merged = (first.astype(jnp.float32) + upward).astype(jnp.bfloat16)
    predicted = jnp.dot(merged, w_out, preferred_element_type=jnp.float32)
    error = predicted - noise_patch.reshape(side * side, chans).astype(jnp.float32)
    return jnp.sum(error * error) / (2.0 * chans)


def patch_grads(window_feat, window_noise, start, sigma, weights, live):
    side = window_feat.shape[0]
    feat = lax.dynamic_slice_in_dim(window_feat, start, side, 1).astype(jnp.float32)
    noise_patch = lax.dynamic_slice_in_dim(window_noise, start, side, 1)

    def local_loss(feat_in, conv_in, down_in, up_in, out_in):
        return patch_loss(feat_in, noise_patch, sigma, conv_in, down_in, up_in, out_in)

    value, pull = jax.vjp(local_loss, feat, *weights)
    return (value * live, pull(live))


def run_slots(window_feat, window_noise, starts, sigmas, lives, weights):
    side = window_feat.shape[0]

    def one_slot(inner, slot):
        grad_win, sums = inner
        start = starts[slot]
        value, grads = patch_grads(
            window_feat, window_noise, start, sigmas[slot], weights, lives[slot]
        )
        current = lax.dynamic_slice_in_dim(grad_win, start, side, 1)
        grad_win = lax.dynamic_update_slice_in_dim(grad_win, current + grads[0], start, 1)
        sums = tuple(
            (total + part.astype(jnp.float32) for total, part in zip(sums[:4], grads[1:]))
        ) + (sums[4] + value,)
        return ((grad_win, sums), None)

    empty = jnp.zeros(window_feat.shape, jnp.float32)
    init = tuple((jnp.zeros(w.shape, jnp.float32) for w in weights)) + (jnp.zeros((), jnp.float32),)
    (grad_win, sums), unused = lax.scan(
        one_slot, (empty, init), jnp.arange(starts.shape[0], dtype=jnp.int32)
    )
    return (grad_win, sums)


def per_device(encoder_features, noise, patch_cols, timesteps, w_conv, w_down, w_up, w_out):
    weights = (w_conv, w_down, w_up, w_out)
    side = encoder_features.shape[0]
    block_cols = encoder_features.shape[1]
    lon_index = lax.axis_index("lon")
    band_starts = patch_cols[0]
    band_levels = timesteps[0]
    band_patches = band_starts.shape[0]
    neighbor = shifted((encoder_features, noise), "lon", -1)
    window_feat = jnp.concatenate([encoder_features, neighbor[0]], axis=1)
    window_noise = jnp.concatenate([noise, neighbor[1]], axis=1)
    owners = band_starts // block_cols
    is_mine = owners == lon_index
    positions = jnp.arange(band_patches, dtype=jnp.int32)
    sort_key = jnp.where(is_mine, 0, band_patches) + positions
    picked = jnp.argsort(sort_key)[:PMAX]
    lives = is_mine[picked].astype(jnp.float32)
    starts = jnp.clip(band_starts[picked] - lon_index * block_cols, 0, block_cols)
    grad_win, sums = run_slots(
        window_feat, window_noise, starts, sigma_of(band_levels[picked]), lives, weights
    )
    returned = shifted(grad_win[:, block_cols:].astype(jnp.bfloat16), "lon", 1).astype(jnp.float32)
    feature_grad = grad_win[:, :block_cols] + returned
    totals = lax.psum((sums[0], sums[1], sums[2], sums[3], sums[4]), ("lat", "lon"))
    loss_value = totals[4] / (lax.axis_size("lat") * band_patches * side * side)
    return (feature_grad, totals[0], totals[1], totals[2], totals[3], loss_value)


def solution(mesh):
    placed = (
        P("lat", "lon", None),
        P("lat", "lon", None),
        P("lat", None),
        P("lat", None),
        P(),
        P(),
        P(),
        P(),
    )
    return jax.shard_map(
        per_device,
        mesh=mesh,
        in_specs=placed,
        out_specs=(P("lat", "lon", None), P(), P(), P(), P(), P()),
        check_vma=False,
    )
```

profile of v0, /device:TPU:1, one launch (start us, length us, event | category | flops | bytes accessed | tf_op | source)
XLA Modules:
  0.0 559.0 jit_solution(14067091899618015423)
XLA Ops:
  8.6 2.3 collective-permute-start.1
  18.8 370.3 %while.23 = (s32[]{:T(128)}, f32[32,64,128]{2,1,0:T(8,128)S(1)}, f32[1152,128]{1,0:T(8,128)}, f32[512,256]{1,0:T(8,128)S(1)}, f32[256,512]{1,0:T(8,128)}, /*inde...) while((s32[]{:T(128)}, f32[32,64,128]{2,1,0:T(8,128)S(1)}, ...), condition=%wide.region_3.4_spmd.clone, body=%wide.region_1.3_spmd.clone.sunk | while | flops 1422756864 | bytes 64128688 | solution.py:95
  25.8 2.0 multiply_convert_fusion.11
  36.5 2.0 fusion.115
  40.8 2.9 fusion.113
  43.7 2.0 convolution_convert_fusion.11
  56.6 2.0 multiply_convert_fusion.11
  67.3 2.2 fusion.115
  71.8 2.9 fusion.113
  74.7 2.0 convolution_convert_fusion.11
  87.6 1.9 multiply_convert_fusion.11
  98.2 2.2 fusion.115
  102.7 2.9 fusion.113
  105.6 2.0 convolution_convert_fusion.11
  129.0 2.2 fusion.115
  133.6 2.9 fusion.113
  136.4 2.0 convolution_convert_fusion.11
  149.3 1.9 multiply_convert_fusion.11
  159.9 2.2 fusion.115
  164.4 2.9 fusion.113
  167.3 2.0 convolution_convert_fusion.11
  180.2 1.9 multiply_convert_fusion.11
  190.8 2.2 fusion.115
  195.3 2.9 fusion.113
  198.1 2.0 convolution_convert_fusion.11
  211.1 1.9 multiply_convert_fusion.11
  221.6 2.2 fusion.115
  226.1 2.9 fusion.113
  229.0 2.0 convolution_convert_fusion.11
  241.9 1.9 multiply_convert_fusion.11
  252.5 2.2 fusion.115
  257.0 2.9 fusion.113
  259.9 2.0 convolution_convert_fusion.11
  283.3 2.2 fusion.115
  287.8 2.9 fusion.113
  290.7 2.0 convolution_convert_fusion.11
  314.2 2.2 fusion.115
  318.7 2.9 fusion.113
  321.6 2.0 convolution_convert_fusion.11
  345.0 2.2 fusion.115
  349.5 2.9 fusion.113
  352.4 2.0 convolution_convert_fusion.11
  375.9 2.2 fusion.115
  380.4 2.9 fusion.113
  383.3 2.0 convolution_convert_fusion.11
  391.2 70.1 %psum.39 = f32[]{:T(128)} all-reduce(f32[]{:T(128)} %get-tuple-element.593), channel_id=1, replica_groups=mesh['lat'=16,'lon'=8] {'lat','lon'}, use_global_device_ids=true, to_apply=%region_8.9 | all-reduce | flops 1 | bytes 8 | tf_op jit(solution)/shard_map/psum | solution.py:124
  462.9 82.9 %all-reduce.13.cloned.1.call-done = (f32[1152,128]{1,0:T(8,128)}, f32[512,256]{1,0:T(8,128)}, f32[256,512]{1,0:T(8,128)}, f32[128,128]{1,0:T(8,128)}) async-done(((f32[1152,128]{1,0:T(8,128)}, f32[512,256]{1,0:T(8,128)}, f32[256,512]{1,0:T(8,128)}, f32[128,128]{1,0:T(8,128)}), (f32[1152,128]{1,0:T(8,128)}, f32[512,256]{1,0:T(8,128)}, f32[256,512]{1,0:T(8,128)}, ...) | async-done | bytes 1703952 | tf_op jit(solution)/shard_map/psum | solution.py:124
  545.8 2.0 copy.68
  (668 shorter events, 198.7 us)
Async XLA Ops:
  7.2 6.1 %copy-start = (s32[1,32]{1,0:T(1,128)S(1)}, s32[1,32]{1,0:T(1,128)}, u32[]{:S(2)}) copy-start(s32[1,32]{1,0:T(1,128)} %param.13) | copy-start | bytes 388
  7.2 10.6 %copy-start.11 = (bf16[32,32,128]{2,1,0:T(8,128)(2,1)S(1)}, bf16[32,32,128]{2,1,0:T(8,128)(2,1)}, u32[]{:S(2)}) copy-start(bf16[32,32,128]{2,1,0:T(8,128)(2,1)} %param.11) | copy-start | bytes 786436
  7.2 538.6 %all-reduce.13.cloned.1.call-start = ((), (), s32[]{:S(2)}) async-start(), calls=%async_computation | async-start | bytes 3407872 | tf_op jit(solution)/shard_map/psum | solution.py:124
  7.2 8.8 %collective-permute-start = (bf16[32,32,128]{2,1,0:T(8,128)(2,1)}, bf16[32,32,128]{2,1,0:T(8,128)(2,1)S(1)}, u32[]{:S(2)}, u32[]{:S(2)}) collective-permute-start(bf16[32,32,128]{2,1,0:T(8,128)(2,1)} %param.10), channel_id=1, source_target_pairs={{1,0},{2,1},{3,2},{4,3},{5,4},{6,5},{7,6},{0,7},{9,8},{10,9},{11,1... | collective-permute-start | bytes 786440 | tf_op jit(solution)/shard_map/ppermute | solution.py:19
  8.6 9.2 %collective-permute-start.1 = (bf16[32,32,128]{2,1,0:T(8,128)(2,1)}, bf16[32,32,128]{2,1,0:T(8,128)(2,1)S(1)}, u32[]{:S(2)}, u32[]{:S(2)}) collective-permute-start(bf16[32,32,128]{2,1,0:T(8,128)(2,1)} %param.11), channel_id=1, source_target_pairs={{1,0},{2,1},{3,2},{4,3},{5,4},{6,5},{7,6},{0,7},{9,8},{10,9},{11,1... | collective-permute-start | bytes 786440 | tf_op jit(solution)/shard_map/ppermute | solution.py:19
  13.2 5.6 copy-start.1
  13.2 5.6 copy-start.5
  13.3 5.6 copy-start.13
  13.3 5.6 copy-start.15
  40.8 2.9 copy-start.17
  46.2 3.5 copy-start.14
  46.2 3.5 copy-start.16
  71.8 2.9 copy-start.17
  77.1 3.5 copy-start.14
  77.2 3.5 copy-start.16
  102.7 2.9 copy-start.17
  108.1 3.4 copy-start.14
  108.1 3.4 copy-start.16
  133.6 2.9 copy-start.17
  138.9 3.4 copy-start.14
  138.9 3.4 copy-start.16
  164.4 2.9 copy-start.17
  169.8 3.4 copy-start.14
  169.8 3.4 copy-start.16
  195.3 2.9 copy-start.17
  200.6 3.4 copy-start.14
  200.6 3.4 copy-start.16
  226.1 2.9 copy-start.17
  231.5 3.4 copy-start.14
  231.5 3.4 copy-start.16
  257.0 2.9 copy-start.17
  262.3 3.4 copy-start.14
  262.3 3.4 copy-start.16
  287.8 2.9 copy-start.17
  293.2 3.4 copy-start.14
  293.2 3.4 copy-start.16
  318.7 2.9 copy-start.17
  324.0 3.4 copy-start.14
  324.1 3.4 copy-start.16
  349.5 2.9 copy-start.17
  354.9 3.4 copy-start.14
  354.9 3.4 copy-start.16
  380.4 2.9 copy-start.17
  385.8 3.4 copy-start.14
  385.8 3.4 copy-start.16
  390.1 71.9 %collective-permute-start.2 = (bf16[32,32,128]{2,1,0:T(8,128)(2,1)S(1)}, bf16[32,32,128]{2,1,0:T(8,128)(2,1)S(1)}, u32[]{:S(2)}, u32[]{:S(2)}) collective-permute-start(bf16[32,32,128]{2,1,0:T(8,128)(2,1)S(1)} %slice.108), channel_id=1, source_target_pairs={{7,0},{0,1},{1,2},{2,3},{3,4},{4,5},{5,6},{6,7},{15,8},{8,9},{9,10... | collective-permute-start | bytes 786440 | tf_op jit(solution)/shard_map/ppermute | solution.py:19
  545.8 3.9 copy-start.10
  545.8 4.6 copy-start.12
  (62 other events, 105.4 us)
Sparse Core Ops, SparseCore 0:
  390.1 155.5 all-reduce.12
where the time goes:
time: 563 us; the launch traced here: 559 us
  matrix products  148 us (26%)
  local copies, waits for them, and re-layouts  96.5 us (17%)
  loops' own time  89.1 us (16%)
  waiting for transfers between devices  82.9 us (15%)
  blocking collectives  70.1 us (12%)
  other arithmetic  52 us (9%)
  between operations  16 us (3%)
    another operation x1, loops' own time, run_slots(): lax.scan(one_slot, (empty, init), jnp.arange(starts.shape[0], dtype=jnp.i...  89.1 us
    psum x1, waiting for transfers between devices, per_device(): lax.psum((sums[0], sums[1], sums[2], sums[3], sums[4]), ('lat', 'lon'))  82.9 us
    dot_general x36, matrix products, patch_loss(): jnp.dot(stacked, w_conv, preferred_element_type=jnp.float32)  77.3 us
    psum x1, blocking collectives, per_device(): lax.psum((sums[0], sums[1], sums[2], sums[3], sums[4]), ('lat', 'lon'))  70.1 us
    dot_general x36, matrix products, patch_loss(): jnp.dot(coarse, w_up, preferred_element_type=jnp.float32)  43.7 us
    convert_element_type x12, other arithmetic, patch_loss(): (scale_in * (feat + sigma * noise_patch.astype(jnp.float32))).astype(jnp....  23.1 us
    while x288, local copies, waits for them, and re-layouts  19.7 us
    dot_general x36, matrix products, patch_loss(): predicted = jnp.dot(merged, w_out, preferred_element_type=jnp.float32)  16.8 us
  transfers between devices with their start and end apart: 4, of which 1 were waited for; matrix products, arithmetic and copies ran while one was open for 1% of the time, Pallas kernels for 0%

commit v1 on v0

v1 whole, which is shorter than its diff:
```python
import math

import jax
import jax.numpy as jnp
from jax import lax
from jax.experimental import pallas as pl
from jax.experimental.pallas import tpu as pltpu
from jax.sharding import PartitionSpec as P

NSTEPS = 32
SIGMA_LOW = 0.02
SIGMA_HIGH = 20.0

SIDE = 32
HALF = SIDE // 2
GROUP = 8
M = GROUP * SIDE
MH = M // 2
OWN = 4
HALO = OWN + 2
CH = 128
INTERPRET = False

ROWS_CONV = 9 * CH
ROWS_DOWN = ROWS_CONV + 1024
ROWS_UP = ROWS_DOWN + 1024
ROWS_OUT = ROWS_UP + CH
ROWS_ALL = ROWS_OUT + 8

F32 = jnp.float32
BF16 = jnp.bfloat16


def mm(a, b, dims):
    return lax.dot_general(a, b, (dims, ((), ())), preferred_element_type=F32)


NN = ((1,), (0,))
NT = ((1,), (1,))
TN = ((0,), (0,))


def shift_cols(even, odd, place):
    down = pltpu.roll(odd.astype(F32), 1, 0)
    up = pltpu.roll(even.astype(F32), MH - 1, 0)
    down = jnp.where(place == 0, 0.0, down).astype(BF16)
    up = jnp.where(place == HALF - 1, 0.0, up).astype(BF16)
    return down, up


def band_kernel(
    cols_ref, rows_ref, scale_ref, sigma_ref, feat_ref, noise_ref,
    w_conv_ref, w_back_ref, w_down_ref, w_up_ref, w_out_ref,
    grad_ref, sums_ref,
    a_ref, ci_ref, d3_ref, du_ref, df_ref, fg_ref, gc_ref, gd_ref, loss_ref,
):
    step = pl.program_id(0)
    last = pl.num_programs(0) - 1
    nlon = feat_ref.shape[0]

    @pl.when(step == 0)
    def _():
        fg_ref[...] = jnp.zeros_like(fg_ref)
        gc_ref[...] = jnp.zeros_like(gc_ref)
        gd_ref[...] = jnp.zeros_like(gd_ref)
        loss_ref[...] = jnp.zeros_like(loss_ref)
        sums_ref[...] = jnp.zeros_like(sums_ref)

    scale = scale_ref[...]
    sigma = sigma_ref[...]
    pick = (lax.broadcasted_iota(jnp.int32, (M, nlon), 1) == cols_ref[...]).astype(F32).astype(BF16)
    feat = mm(pick, feat_ref[...], NN)
    noise = mm(pick, noise_ref[...], NN)
    hidden = (scale * (feat + sigma * noise)).astype(BF16)
    place_wide = lax.broadcasted_iota(jnp.int32, (MH, HALO * CH), 0) % HALF
    place = lax.broadcasted_iota(jnp.int32, (MH, CH), 0) % HALF

    even, odd = hidden[:MH], hidden[MH:]
    down, up = shift_cols(even, odd, place_wide)
    for r in range(OWN):
        for dr in range(3):
            src = slice((r + dr) * CH, (r + dr + 1) * CH)
            k = dr * 3 * CH
            a_ref[r * M : r * M + MH, k : k + CH] = down[:, src]
            a_ref[r * M + MH : (r + 1) * M, k : k + CH] = even[:, src]
            a_ref[r * M : (r + 1) * M, k + CH : k + 2 * CH] = hidden[:, src]
            a_ref[r * M : r * M + MH, k + 2 * CH : k + 3 * CH] = odd[:, src]
            a_ref[r * M + MH : (r + 1) * M, k + 2 * CH : k + 3 * CH] = up[:, src]

    pre = mm(a_ref[...], w_conv_ref[...], NN)
    gate = jax.nn.sigmoid(pre)
    first = (pre * gate).astype(BF16)
    slope = gate * (1.0 + pre * (1.0 - gate))

    for i in range(2):
        for k in range(4):
            start = (2 * i + k // 2) * M + (k % 2) * MH
            ci_ref[i * MH : (i + 1) * MH, k * CH : (k + 1) * CH] = first[start : start + MH]
    pre2 = mm(ci_ref[...], w_down_ref[...], NN)
    gate2 = jax.nn.sigmoid(pre2)
    coarse = (pre2 * gate2).astype(BF16)
    slope2 = gate2 * (1.0 + pre2 * (1.0 - gate2))
    upward = mm(coarse, w_up_ref[...], NN)

    spread = []
    for r in range(OWN):
        for q in range(2):
            k = (r % 2) * 2 + q
            spread.append(upward[(r // 2) * MH : (r // 2 + 1) * MH, k * CH : (k + 1) * CH])
    merged = (first.astype(F32) + jnp.concatenate(spread, axis=0)).astype(BF16)
    target = jnp.concatenate([noise[:, (r + 1) * CH : (r + 2) * CH] for r in range(OWN)], axis=0)
    error = mm(merged, w_out_ref[...], NN) - target
    loss_ref[...] += jnp.sum((error * error).reshape(-1, 8, CH), axis=0)
    d_pred = (error * (2.0 / (2.0 * CH))).astype(BF16)

    sums_ref[ROWS_UP:ROWS_OUT, :] += mm(merged, d_pred, TN)
    d_merged = mm(d_pred, w_out_ref[...], NT).astype(BF16)
    for i in range(2):
        for k in range(4):
            start = (2 * i + k // 2) * M + (k % 2) * MH
            du_ref[i * MH : (i + 1) * MH, k * CH : (k + 1) * CH] = d_merged[start : start + MH]
    d_up = du_ref[...]
    g_up = mm(coarse, d_up, TN)
    for k in range(4):
        sums_ref[ROWS_DOWN + k * 256 : ROWS_DOWN + (k + 1) * 256, :] += g_up[:, k * CH : (k + 1) * CH]
    d_coarse = mm(d_up, w_up_ref[...], NT).astype(BF16).astype(F32)
    d_pre2 = (d_coarse * slope2).astype(BF16)
    gd_ref[...] += mm(d_pre2, ci_ref[...], TN)
    d_ci = mm(d_pre2, w_down_ref[...], NT)
    spread = []
    for r in range(OWN):
        for q in range(2):
            k = (r % 2) * 2 + q
            spread.append(d_ci[(r // 2) * MH : (r // 2 + 1) * MH, k * CH : (k + 1) * CH])
    d_first = d_merged.astype(F32) + jnp.concatenate(spread, axis=0)
    d_pre = (d_first * slope).astype(BF16)
    gc_ref[...] += mm(d_pre, a_ref[...], TN)

    for r in range(OWN):
        even, odd = d_pre[r * M : r * M + MH], d_pre[r * M + MH : (r + 1) * M]
        down, up = shift_cols(even, odd, place)
        k = r * 3 * CH
        d3_ref[:MH, k : k + CH] = odd
        d3_ref[MH:, k : k + CH] = up
        d3_ref[:MH, k + CH : k + 2 * CH] = even
        d3_ref[MH:, k + CH : k + 2 * CH] = odd
        d3_ref[:MH, k + 2 * CH : k + 3 * CH] = down
        d3_ref[MH:, k + 2 * CH : k + 3 * CH] = even
    for r in range(HALO):
        lo, hi = max(0, r - 2), min(OWN - 1, r)
        wlo = (2 - (r - lo)) * 3 * CH
        width = (hi - lo + 1) * 3 * CH
        d_hidden = mm(
            d3_ref[:, lo * 3 * CH : lo * 3 * CH + width], w_back_ref[wlo : wlo + width, :], NN
        ).astype(BF16)
        df_ref[:, r * CH : (r + 1) * CH] = (scale * d_hidden.astype(F32)).astype(BF16)
    put = (lax.broadcasted_iota(jnp.int32, (nlon, M), 0) == rows_ref[0]).astype(F32).astype(BF16)
    fg_ref[...] += mm(put, df_ref[...], NN)

    @pl.when(step == last)
    def _():
        grad_ref[...] = fg_ref[...].astype(BF16)
        sums_ref[:ROWS_CONV, :] = gc_ref[...].T
        g_down = gd_ref[...].T
        sums_ref[ROWS_CONV : ROWS_CONV + 512, :] = g_down[:, :CH]
        sums_ref[ROWS_CONV + 512 : ROWS_DOWN, :] = g_down[:, CH:]
        sums_ref[ROWS_OUT:, :] = loss_ref[...]


def run_band(cols, scale, sigma, feat, noise, w_conv, w_back, w_down, w_up, w_out):
    steps = cols.shape[0] // M
    nlon = feat.shape[0]

    def whole(array):
        return pl.BlockSpec(array.shape, lambda g: (0,) * array.ndim)

    column = pl.BlockSpec((M, 1), lambda g: (g, 0))
    rows = cols.reshape(steps, 1, M)
    return pl.pallas_call(
        band_kernel,
        grid=(steps,),
        in_specs=[column, pl.BlockSpec((1, 1, M), lambda g: (g, 0, 0)), column, column]
        + [whole(x) for x in (feat, noise, w_conv, w_back, w_down, w_up, w_out)],
        out_specs=[
            pl.BlockSpec((nlon, HALO * CH), lambda g: (0, 0)),
            pl.BlockSpec((ROWS_ALL, CH), lambda g: (0, 0)),
        ],
        out_shape=[
            jax.ShapeDtypeStruct((nlon, HALO * CH), BF16),
            jax.ShapeDtypeStruct((ROWS_ALL, CH), F32),
        ],
        scratch_shapes=[
            pltpu.VMEM((OWN * M, 9 * CH), BF16),
            pltpu.VMEM((2 * MH, 4 * CH), BF16),
            pltpu.VMEM((M, OWN * 3 * CH), BF16),
            pltpu.VMEM((2 * MH, 4 * CH), BF16),
            pltpu.VMEM((M, HALO * CH), BF16),
            pltpu.VMEM((nlon, HALO * CH), F32),
            pltpu.VMEM((CH, 9 * CH), F32),
            pltpu.VMEM((2 * CH, 4 * CH), F32),
            pltpu.VMEM((8, CH), F32),
        ],
        interpret=INTERPRET,
    )(cols, rows, scale, sigma, feat, noise, w_conv, w_back, w_down, w_up, w_out)


def rows_for_devices(block, count):
    padded = jnp.pad(block, ((1, 1), (0, 0), (0, 0)))
    parts = jnp.stack([padded[OWN * d : OWN * d + HALO] for d in range(count)])
    return parts.transpose(0, 2, 1, 3).reshape(count, block.shape[1], HALO * CH)


def reduce_sums(sums):
    return lax.psum(sums, ("lat", "lon"))


def per_device(encoder_features, noise, patch_cols, timesteps, w_conv, w_down, w_up, w_out):
    count = lax.axis_size("lon")
    block_cols = encoder_features.shape[1]
    nlon = count * block_cols
    starts = patch_cols[0]
    patches = starts.shape[0]
    sigmas = SIGMA_LOW * jnp.exp(
        timesteps[0].astype(F32) / (NSTEPS - 1) * math.log(SIGMA_HIGH / SIGMA_LOW)
    )
    scales = 1.0 / jnp.sqrt(1.0 + sigmas * sigmas)

    sent = jnp.concatenate(
        [rows_for_devices(encoder_features, count), rows_for_devices(noise, count)], axis=1
    )
    got = lax.all_to_all(sent, "lon", 0, 0, tiled=True)
    feat_rows = got[:, :block_cols].reshape(nlon, HALO * CH)
    noise_rows = got[:, block_cols:].reshape(nlon, HALO * CH)

    groups = patches // GROUP
    offsets = jnp.arange(2)[None, :, None, None] + 2 * jnp.arange(HALF)[None, None, None, :]
    shape = (groups, 2, GROUP, HALF)

    def per_column(values):
        return jnp.broadcast_to(values.reshape(groups, 1, GROUP, 1), shape).reshape(-1, 1)

    cols = ((starts.reshape(groups, 1, GROUP, 1) + offsets) % nlon).astype(jnp.int32)
    w_back = w_conv.reshape(3, 3, CH, CH)[::-1].transpose(0, 1, 3, 2).reshape(9 * CH, CH)
    grad, sums = run_band(
        cols.reshape(-1, 1), per_column(scales), per_column(sigmas),
        feat_rows, noise_rows, w_conv, w_back, w_down, w_up, w_out,
    )

    back = lax.all_to_all(grad.reshape(count, block_cols, HALO * CH), "lon", 0, 0, tiled=True)
    back = back.reshape(count, block_cols, HALO, CH).transpose(0, 2, 1, 3).astype(F32)
    zero = jnp.zeros_like(back[:1, 0])
    above = jnp.concatenate([zero, back[:-1, HALO - 1]], axis=0)
    below = jnp.concatenate([back[1:, 0], zero], axis=0)
    own = back[:, 1 : OWN + 1]
    feature_grad = jnp.concatenate(
        [own[:, :1] + above[:, None], own[:, 1 : OWN - 1], own[:, OWN - 1 :] + below[:, None]],
        axis=1,
    ).reshape(encoder_features.shape)

    total = reduce_sums(sums)
    grad_conv = total[:ROWS_CONV]
    grad_down = jnp.concatenate(
        [total[ROWS_CONV : ROWS_CONV + 512], total[ROWS_CONV + 512 : ROWS_DOWN]], axis=1
    )
    grad_up = jnp.concatenate(
        [total[ROWS_DOWN + k * 256 : ROWS_DOWN + (k + 1) * 256] for k in range(4)], axis=1
    )
    grad_out = total[ROWS_UP:ROWS_OUT]
    cells = lax.axis_size("lat") * patches * SIDE * SIDE
    loss_value = jnp.sum(total[ROWS_OUT:]) / (2.0 * CH) / cells
    return (feature_grad, grad_conv, grad_down, grad_up, grad_out, loss_value)


def solution(mesh):
    placed = (P("lat", "lon", None), P("lat", "lon", None), P("lat", None), P("lat", None))
    return jax.shard_map(
        per_device,
        mesh=mesh,
        in_specs=placed + (P(), P(), P(), P()),
        out_specs=(P("lat", "lon", None), P(), P(), P(), P(), P()),
        check_vma=False,
    )
```

time: 563 us -> 237 us (0.42)
  matrix products: 148 us -> 0 us
  loops' own time: 89.1 us -> 0 us
  waiting for transfers between devices: 82.9 us -> 161 us
  local copies, waits for them, and re-layouts: 96.5 us -> 18.7 us
  blocking collectives: 70.1 us -> 0 us
  other arithmetic: 52 us -> 7.01 us
  Pallas kernels: 0 us -> 22.8 us
    dot_general x144 -> x0, matrix products: 148 us -> none  [the longest x36 77.3 us: patch_loss(): jnp.dot(stacked, w_conv, preferred_element_type=jnp.float32)]
    another operation x1 -> x0, loops' own time: 89.1 us -> none  [run_slots(): lax.scan(one_slot, (empty, init), jnp.arange(starts.shape[0], dtype=jnp.i...]
    psum x1 -> x0, blocking collectives: 70.1 us -> none  [per_device(): lax.psum((sums[0], sums[1], sums[2], sums[3], sums[4]), ('lat', 'lon'))]
    psum x1, waiting for transfers between devices: 82.9 us -> 148 us  [reduce_sums(): return lax.psum(sums, ('lat', 'lon'))]
    convert_element_type x25 -> x0, other arithmetic: 35.6 us -> none  [the longest x12 23.1 us: patch_loss(): (scale_in * (feat + sigma * noise_patch.astype(jnp.float32))).astype(jnp....]
    dynamic_slice x48 -> x0, local copies, waits for them, and re-layouts: 28.8 us -> none  [the longest x12 7.64 us: one_slot(): lives[slot]]
    pallas_call x0 -> x1, Pallas kernels: none -> 22.8 us  [run_band(): pl.pallas_call(band_kernel, grid=(steps,), in_specs=[column, pl.BlockSpec...]
    while x288 -> x0, local copies, waits for them, and re-layouts: 19.7 us -> none
  transfers between devices with their start and end apart: 4 -> 3, of which waited for: 1 -> 3; matrix products, arithmetic and copies ran while one was open for 1% -> 4% of each run, Pallas kernels for 0% -> 0%
where the time goes in v1:
time: 237 us; the launch traced here: 236 us
  waiting for transfers between devices  161 us (68%)
  Pallas kernels  22.8 us (10%)
  local copies, waits for them, and re-layouts  18.7 us (8%)
  between operations  16 us (7%)
  starting transfers between devices  10.1 us (4%)
  other arithmetic  7.01 us (3%)
    psum x1, waiting for transfers between devices, reduce_sums(): return lax.psum(sums, ('lat', 'lon'))  148 us
    pallas_call x1, Pallas kernels, run_band(): pl.pallas_call(band_kernel, grid=(steps,), in_specs=[column, pl.BlockSpec...  22.8 us
    unnamed x25, local copies, waits for them, and re-layouts  8.66 us
    all_to_all x1, waiting for transfers between devices, per_device(): lax.all_to_all(grad.reshape(count, block_cols, HALO * CH), 'lon', 0, 0, t...  7 us
    all_to_all x1, starting transfers between devices, per_device(): got = lax.all_to_all(sent, 'lon', 0, 0, tiled=True)  5.79 us
    all_to_all x1, waiting for transfers between devices, per_device(): got = lax.all_to_all(sent, 'lon', 0, 0, tiled=True)  5.24 us
  transfers between devices with their start and end apart: 3, of which 3 were waited for; matrix products, arithmetic and copies ran while one was open for 4% of the time, Pallas kernels for 0%

profile of v1, /device:TPU:1, one launch (start us, length us, event | category | flops | bytes accessed | tf_op | source)
XLA Modules:
  0.0 235.9 jit_solution(9320164382420635684)
XLA Ops:
  7.2 0.8 fusion.2
  8.0 0.8 bitcast_dynamic-update-slice_fusion.11
  8.8 0.8 bitcast_dynamic-update-slice_fusion.10
  9.6 0.8 bitcast_dynamic-update-slice_fusion.9
  10.4 0.8 bitcast_dynamic-update-slice_fusion.8
  11.2 0.8 bitcast_dynamic-update-slice_fusion.7
  12.0 0.8 bitcast_dynamic-update-slice_fusion.6
  12.9 0.8 fusion.4
  13.6 0.8 fusion.6
  14.4 0.8 bitcast_dynamic-update-slice_fusion.5
  15.2 0.8 bitcast_dynamic-update-slice_fusion.4
  16.2 0.9 pad_maximum_fusion
  17.2 5.8 %all-to-all-start = ((bf16[8,64,768]{2,1,0:T(8,128)(2,1)}), bf16[8,64,768]{2,1,0:T(8,128)(2,1)S(1)}, u32[]{:S(2)}, u32[]{:S(2)}) async-start(bf16[8,64,768]{2,1,0:T(8,128)(2,1)} %pad_maximum_fusion), calls=%async_computation | async-start | bytes 1572864 | tf_op jit(solution)/shard_map/all_to_all | solution.py:231
  23.0 0.1 mul.52
  23.1 0.5 broadcast.173
  23.6 0.7 reduce.7
  24.3 0.1 add.111
  24.3 0.1 add.122
  24.4 0.1 broadcast_add_fusion
  24.5 0.1 add.112
  24.6 0.1 add.120
  24.7 0.2 copy.35
  24.9 0.7 rev.3
  25.6 0.3 add.129
  25.9 0.1 broadcast_in_dim.8
  26.0 1.1 reshape.232.scale_ref
  27.2 1.1 reshape.233.sigma_ref
  28.3 0.6 and_select_fusion.rows_ref
  28.9 1.0 add_select_fusion.cols_ref
  29.9 5.2 %all-to-all-done = bf16[8,64,768]{2,1,0:T(8,128)(2,1)S(1)} async-done(((bf16[8,64,768]{2,1,0:T(8,128)(2,1)}), bf16[8,64,768]{2,1,0:T(8,128)(2,1)S(1)}, u32[]{:S(2)}, u32[]{:S(2)}) %all-to-all-start) | async-done | bytes 786464 | tf_op jit(solution)/shard_map/all_to_all | solution.py:231
  35.1 0.9 fusion.13
  36.0 22.8 %shard_map.127 = (bf16[256,768]{1,0:T(8,128)(2,1)}, f32[3336,128]{1,0:T(8,128)}) custom-call(s32[1024,1]{1,0:T(8,128)} %add_select_fusion.cols_ref, s32[4,1,256]{2,1,0:T(1,128)} %and_select_fusion.rows_ref, f32[1024,1]{1,0:T(8,128)} %reshape.232.scale_ref, f32[1024,1]{1,0:T(8,128)} %reshape.233.sigma_ref, bf16[256,768]{1,0:T(8,128)(2,1)} %bitcast.82, ...), custom_call_target="tpu_custom_call" | custom-call | tf_op jit(solution)/shard_map/pallas_call | solution.py:179
  58.9 4.3 %all-to-all-start.1 = ((bf16[8,32,768]{2,1,0:T(8,128)(2,1)}), bf16[8,32,768]{2,1,0:T(8,128)(2,1)S(1)}, u32[]{:S(2)}, u32[]{:S(2)}) async-start(bf16[8,32,768]{2,1,0:T(8,128)(2,1)} %bitcast.91), calls=%async_computation.1 | async-start | bytes 786432 | tf_op jit(solution)/shard_map/all_to_all | solution.py:249
  63.2 0.7 all-reduce.6.cloned.1.call-update
  63.9 7.0 %all-to-all-done.1 = bf16[8,32,768]{2,1,0:T(8,128)(2,1)S(1)} async-done(((bf16[8,32,768]{2,1,0:T(8,128)(2,1)}), bf16[8,32,768]{2,1,0:T(8,128)(2,1)S(1)}, u32[]{:S(2)}, u32[]{:S(2)}) %all-to-all-start.1) | async-done | bytes 393248 | tf_op jit(solution)/shard_map/all_to_all | solution.py:249
  70.9 0.4 reshape.231
  71.3 0.1 slice.148
  71.5 0.2 fusion.12
  71.7 0.3 slice_add_fusion
  72.0 0.4 pad_maximum_fusion.1
  72.4 0.9 copy.41
  73.3 148.4 %all-reduce.6.cloned.1.call-done = f32[3336,128]{1,0:T(8,128)} async-done(((f32[3336,128]{1,0:T(8,128)}), f32[3336,128]{1,0:T(8,128)}) %all-reduce.6.cloned.1.call-update) | async-done | bytes 1708048 | tf_op jit(solution)/shard_map/psum | solution.py:214
  221.6 1.4 slice_reduce_fusion
  223.7 1.1 fusion.11
  224.8 0.8 pad_maximum_fusion.2
  225.6 0.8 pad_maximum_fusion.3
  226.5 0.6 slice.158
  227.1 0.9 slice.151
  (26 shorter events, 0.3 us)
Async XLA Ops:
  7.2 8.9 %copy-start = (bf16[32,32,128]{2,1,0:T(8,128)(2,1)S(1)}, bf16[32,32,128]{2,1,0:T(8,128)(2,1)}, u32[]{:S(2)}) copy-start(bf16[32,32,128]{2,1,0:T(8,128)(2,1)} %param.9) | copy-start | bytes 786436
  16.2 6.8 %copy-start.3 = (s32[1,32]{1,0:T(1,128)S(1)}, s32[1,32]{1,0:T(1,128)}, u32[]{:S(2)}) copy-start(s32[1,32]{1,0:T(1,128)} %param.11) | copy-start | bytes 388
  16.2 7.4 %copy-start.4 = (s32[1,32]{1,0:T(1,128)S(1)}, s32[1,32]{1,0:T(1,128)}, u32[]{:S(2)}) copy-start(s32[1,32]{1,0:T(1,128)} %param.10) | copy-start | bytes 388
  16.2 8.4 %copy-start.2 = (bf16[1152,128]{1,0:T(8,128)(2,1)S(1)}, bf16[1152,128]{1,0:T(8,128)(2,1)}, u32[]{:S(2)}) copy-start(bf16[1152,128]{1,0:T(8,128)(2,1)} %w_conv_ref.1) | copy-start | bytes 884740
  17.2 17.9 %all-to-all-start = ((bf16[8,64,768]{2,1,0:T(8,128)(2,1)}), bf16[8,64,768]{2,1,0:T(8,128)(2,1)S(1)}, u32[]{:S(2)}, u32[]{:S(2)}) async-start(bf16[8,64,768]{2,1,0:T(8,128)(2,1)} %pad_maximum_fusion), calls=%async_computation | async-start | bytes 1572864 | tf_op jit(solution)/shard_map/all_to_all | solution.py:231
  58.9 12.0 %all-to-all-start.1 = ((bf16[8,32,768]{2,1,0:T(8,128)(2,1)}), bf16[8,32,768]{2,1,0:T(8,128)(2,1)S(1)}, u32[]{:S(2)}, u32[]{:S(2)}) async-start(bf16[8,32,768]{2,1,0:T(8,128)(2,1)} %bitcast.91), calls=%async_computation.1 | async-start | bytes 786432 | tf_op jit(solution)/shard_map/all_to_all | solution.py:249
  63.2 158.5 %all-reduce.6.cloned.1.call-start = ((), (), s32[]{:S(2)}) async-start(), calls=%async_computation.2 | async-start | bytes 3416064 | tf_op jit(solution)/shard_map/psum | solution.py:214
  221.6 4.0 %copy-start.1 = (f32[3336,128]{1,0:T(8,128)S(1)}, f32[3336,128]{1,0:T(8,128)}, u32[]{:S(2)}) copy-start(f32[3336,128]{1,0:T(8,128)} %all-reduce.6.cloned.1.call-done) | copy-start | bytes 5124100
Sparse Core Ops, SparseCore 0:
  68.8 152.7 all-reduce.5
